TPU v7x, 128 devices: a whole 4x4x4 slice. The times are simulated.
128 devices in a mesh: prow: 4 (over x), pcol: 32 (over y, z, core).
Axes of the slice: x: 4, y: 4, z: 4, core: 2. Of those that a mesh axis runs over, the one named last changes fastest.
Arguments:
- matrix: float32 [128, 4, 128, 1, 32, 128], P(None, 'prow', None, None, 'pcol')
- pivots: int32 [128], replicated, may hold values from 0 to 65535, as said below
Outputs:
- factored: float32 [128, 4, 128, 1, 32, 128], P(None, 'prow', None, None, 'pcol')
Inputs may be any that keep to these rules, and one draw needn't show every extreme that they name: `pivots`: entry j lies between j and 65535; the last entry is 65535.
All inputs are finite; a program needn't handle non-finite values.
Results may differ from a plain program's by a relative error of at most 0.0001.
Values sent between devices are 32-bit elements; how exact they have to be, the bound alone decides.
A program may use at most 128 MiB of HBM per device.

v0:
```python
import jax
import jax.numpy as jnp
from jax import lax
from jax.sharding import PartitionSpec as P


def from_root(value, axis, source):
    kept = jnp.where(lax.axis_index(axis) == source, value, 0).astype(value.dtype)
    return lax.psum(kept, axis)


def eliminate(square):
    size = square.shape[0]
    positions = jnp.arange(size, dtype=jnp.int32)

    def reduce_step(column_no, factors):
        column = factors[:, column_no]
        pivot_value = factors[column_no, column_no]
        below = positions > column_no
        multiplier = jnp.where(below, column / pivot_value, 0.0)
        pivot_row = jnp.where(below, factors[column_no], 0.0)
        factors = factors - multiplier[:, None] * pivot_row[None, :]
        return jnp.where(
            below[:, None] & (positions[None, :] == column_no), multiplier[:, None], factors
        )

    return lax.fori_loop(0, size, reduce_step, square)


def both_inverses(packed):
    size = packed.shape[0]
    positions = jnp.arange(size, dtype=jnp.int32)
    strict_low = jnp.where(positions[:, None] > positions[None, :], packed, 0.0)
    strict_up = jnp.where(positions[:, None] < positions[None, :], packed, 0.0)
    diag_values = jnp.sum(jnp.where(positions[:, None] == positions[None, :], packed, 0.0), axis=1)

    def row_step(step_no, inverses):
        upper_inv, lower_inv = inverses
        low_no = jnp.asarray(step_no).astype(jnp.int32)
        up_no = (size - 1 - jnp.asarray(step_no)).astype(jnp.int32)
        low_row = lax.dynamic_index_in_dim(strict_low, low_no, 0, keepdims=False)
        up_row = lax.dynamic_index_in_dim(strict_up, up_no, 0, keepdims=False)
        pivot_value = lax.dynamic_index_in_dim(diag_values, up_no, 0, keepdims=False)
        low_unit = (positions == low_no).astype(jnp.float32)
        up_unit = (positions == up_no).astype(jnp.float32)
        new_low = low_unit - jnp.dot(
            low_row, lower_inv, precision=lax.Precision.HIGHEST, preferred_element_type=jnp.float32
        )
        new_up = (
            up_unit
            - jnp.dot(
                up_row,
                upper_inv,
                precision=lax.Precision.HIGHEST,
                preferred_element_type=jnp.float32,
            )
        ) / pivot_value
        lower_inv = lax.dynamic_update_index_in_dim(lower_inv, new_low, low_no, 0)
        upper_inv = lax.dynamic_update_index_in_dim(upper_inv, new_up, up_no, 0)
        return (upper_inv, lower_inv)

    start = jnp.zeros((size, size), jnp.float32)
    return lax.fori_loop(0, size, row_step, (start, start))


def global_index(count_items, block_size, group_count, my_place):
    positions = jnp.arange(count_items, dtype=jnp.int32)
    return (positions // block_size * group_count + my_place) * block_size + positions % block_size


def trace_sources(pivots, first_row, count, targets):

    def back_step(step_no, sources):
        column_no = (first_row + count - 1 - step_no).astype(jnp.int32)
        partner = pivots[column_no]
        return jnp.where(
            sources == column_no, partner, jnp.where(sources == partner, column_no, sources)
        )

    return lax.fori_loop(0, count, back_step, targets)


def swap_rows(held, pivots, first_row, count, block_size, prow_count, my_prow):
    rows_local = held.shape[0]
    targets = jnp.concatenate([first_row + jnp.arange(count, dtype=jnp.int32), pivots])
    sources = trace_sources(pivots, first_row, count, targets)
    source_mine = sources // block_size % prow_count == my_prow
    source_local = sources // (block_size * prow_count) * block_size + sources % block_size
    fetched = jnp.take(held, jnp.where(source_mine, source_local, 0), axis=0)
    contrib = jnp.where(source_mine[:, None], fetched, 0.0)
    moved_rows = lax.psum(contrib, "prow")
    target_mine = targets // block_size % prow_count == my_prow
    target_local = targets // (block_size * prow_count) * block_size + targets % block_size
    held = held.at[jnp.where(target_mine, target_local, rows_local)].set(moved_rows, mode="drop")
    return (held, moved_rows)


def local(matrix, pivots):
    row_blocks = matrix.shape[0]
    block_size = matrix.shape[2]
    col_blocks = matrix.shape[3]
    prow_count = lax.axis_size("prow")
    pcol_count = lax.axis_size("pcol")
    my_prow = lax.axis_index("prow")
    my_pcol = lax.axis_index("pcol")
    rows_local = row_blocks * block_size
    cols_local = col_blocks * block_size
    held = matrix.reshape(rows_local, cols_local)
    row_global = global_index(rows_local, block_size, prow_count, my_prow)
    col_global = global_index(cols_local, block_size, pcol_count, my_pcol)
    owner_prow = 0 % prow_count
    row_slot = 0 // prow_count
    owner_pcol = 0 % pcol_count
    col_slot = 0 // pcol_count
    row_lo = row_slot * block_size
    col_lo = col_slot * block_size
    held, moved_rows = swap_rows(held, pivots, 0, block_size, block_size, prow_count, my_prow)
    panel_cols = held
    diag_raw = from_root(
        held[row_lo : row_lo + block_size, col_lo : col_lo + block_size], "prow", owner_prow
    )
    row_raw = held[row_lo : row_lo + block_size]
    below = row_global >= block_size
    packed = eliminate(diag_raw)
    upper_inv, lower_inv = both_inverses(packed)
    solved_cols = jnp.dot(
        panel_cols, upper_inv, precision=lax.Precision.HIGHEST, preferred_element_type=jnp.float32
    )
    payload = jnp.concatenate([jnp.where(below[:, None], solved_cols, 0.0), packed, lower_inv], 0)
    received = from_root(payload, "pcol", owner_pcol)
    left_op = received[:rows_local]
    packed = received[rows_local : rows_local + block_size]
    lower_inv = received[rows_local + block_size :]
    solved = jnp.dot(
        lower_inv, row_raw, precision=lax.Precision.HIGHEST, preferred_element_type=jnp.float32
    )
    row_final = from_root(solved, "prow", owner_prow)
    trailing_cols = col_global >= block_size
    right_op = jnp.where(trailing_cols[None, :], row_final, 0.0)
    held = held - jnp.dot(
        left_op, right_op, precision=lax.Precision.HIGHEST, preferred_element_type=jnp.float32
    )
    panel_new = jnp.where(below[:, None], left_op, panel_cols)
    panel_tiles = panel_new.reshape(row_blocks, block_size, block_size)
    panel_tiles = panel_tiles.at[row_slot].set(
        jnp.where(my_prow == owner_prow, packed, panel_tiles[row_slot])
    )
    held = held.at[:, col_lo : col_lo + block_size].set(
        jnp.where(my_pcol == owner_pcol, panel_tiles.reshape(rows_local, block_size), held)
    )
    keep_rows = (my_prow == owner_prow) & trailing_cols[None, :]
    held = held.at[row_lo : row_lo + block_size].set(
        jnp.where(keep_rows, row_final, held[row_lo : row_lo + block_size])
    )
    return held.reshape(matrix.shape)


def solution(mesh):
    return jax.shard_map(
        local,
        mesh=mesh,
        in_specs=(P(None, "prow", None, None, "pcol", None), P()),
        out_specs=P(None, "prow", None, None, "pcol", None),
        check_vma=False,
    )
```

profile of v0, /device:TPU:0, one launch (start us, length us, event | category | flops | bytes accessed | tf_op | source)
XLA Modules:
  0.0 877.8 jit_solution(12851266730310642802)
XLA Ops:
  6.5 7.0 copy.43
  13.6 150.0 %while.53 = (s32[]{:T(128)}, s32[256]{0:T(256)S(1)}, s32[128]{0:T(128)S(1)}, s32[]{:T(128)}, s32[]{:T(128)}, /*index=5*/s32[]{:T(128)}, s32[]{:T(128)}) while((s32[]{:T(128)}, s32[256]{0:T(256)S(1)}, s32[128]{0:T(128)S(1)}, s32[]{:T(128)}, s32[]{:T(128)}, /*index=5*/s32[]{:T(128)}, s32[]{:T(128)}) %tuple.142), condition=%wide.region_1.2_spmd, body=%wide.region_0.1_spmd.sunk | while | flops 1030 | bytes 2191 | solution.py:80
  163.6 4.1 gather_fusion
  167.7 0.8 select_select_fusion
  168.6 43.9 %all-reduce.5.cloned.1.call-done = f32[256,128]{1,0:T(8,128)} async-done(((f32[256,128]{1,0:T(8,128)}), f32[256,128]{1,0:T(8,128)}) %all-reduce.5.cloned.1.call-update) | async-done | bytes 131088 | tf_op jit(solution)/shard_map/psum | solution.py:91
  212.5 8.2 scatter_fusion
  220.7 1.5 slice_select_fusion.3
  222.3 41.6 %all-reduce.7.cloned.1.call-done = f32[128,128]{1,0:T(8,128)} async-done(((f32[128,128]{1,0:T(8,128)}), f32[128,128]{1,0:T(8,128)}) %all-reduce.7.cloned.1.call-update) | async-done | bytes 65552 | tf_op jit(solution)/shard_map/psum | solution.py:9
  263.9 0.9 copy.4
  264.9 180.8 %while.54 = (s32[]{:T(128)}, f32[128,128]{0,1:T(8,128)S(1)}, s32[]{:T(128)}) while((s32[]{:T(128)}, f32[128,128]{0,1:T(8,128)S(1)}, s32[]{:T(128)}) %tuple.128), condition=%wide.region_6.7_spmd.clone.clone, body=%wide.region_5.6_spmd.clone.clone.sunk | while | flops 66434 | bytes 268349 | solution.py:27
  445.9 197.9 %while.55 = (s32[]{:T(128)}, f32[128,128]{1,0:T(8,128)S(1)}, f32[128,128]{1,0:T(8,128)S(1)}, f32[128,128]{1,0:T(8,128)S(1)}, f32[128]{0:T(128)S(1)}, /*index=5*/...) while((s32[]{:T(128)}, f32[128,128]{1,0:T(8,128)S(1)}, ...), condition=%wide.region_9.10_spmd.clone.clone, body=%wide.region_8.9_spmd.clone.clone.sunk | while | flops 394118 | bytes 136371 | solution.py:63
  446.5 0.7 fusion.73
  448.1 0.7 fusion.73
  643.8 18.9 %convolution_select_fusion = f32[16384,128]{1,0:T(8,128)S(1)} fusion(f32[16384,128]{1,0:T(8,128)} %scatter_fusion, f32[128,128]{1,0:T(8,128)S(1)} %get-tuple-element.386, pred[16384]{0:T(1024)(128)(4,1)S(1)} %fusion.29), kind=kOutput, calls=%fused_computation.32 | convolution fusion | flops 3223322624 | bytes 16859136 | tf_op jit(solution)/shard_map/dot_general | solution.py:126
  662.7 8.7 maximum_select_fusion
  671.8 120.8 %all-reduce.9.cloned.1.call-done = f32[16640,128]{1,0:T(8,128)} async-done(((f32[16640,128]{1,0:T(8,128)}), f32[16640,128]{1,0:T(8,128)}) %all-reduce.9.cloned.1.call-update) | async-done | bytes 8519696 | tf_op jit(solution)/shard_map/psum | solution.py:9
  792.6 9.8 %slice_select_fusion = f32[16384,128]{1,0:T(8,128)S(1)} fusion(f32[16384,128]{1,0:T(8,128)} %scatter_fusion, f32[16640,128]{1,0:T(8,128)} %all-reduce.9.cloned.1.call-done, pred[16384]{0:T(1024)(128)(4,1)S(1)} %fusion.29), kind=kLoop, calls=%fused_computation.35 | loop fusion | flops 2097152 | bytes 25182208 | tf_op jit(solution)/shard_map/jit(_where)/select_n | solution.py:143
  802.5 3.3 copy.39
  805.7 2.5 copy-done
  808.2 1.7 convolution_select_fusion.1
  809.9 1.5 fusion.34
  811.4 39.2 %all-reduce.11.cloned.1.call-done = f32[128,128]{1,0:T(8,128)} async-done(((f32[128,128]{1,0:T(8,128)}), f32[128,128]{1,0:T(8,128)}) %all-reduce.11.cloned.1.call-update) | async-done | bytes 65552 | tf_op jit(solution)/shard_map/psum | solution.py:9
  850.6 17.2 %fusion.17 = f32[16384,128]{1,0:T(8,128)S(1)} fusion(f32[16384,128]{1,0:T(8,128)} %bitcast.90, f32[16384,128]{1,0:T(8,128)} %scatter_fusion, f32[16640,128]{1,0:T(8,128)} %all-reduce.9.cloned.1.call-done, pred[]{:T(512)S(6)} %eq.133, f32[128,128]{1,0:T(8,128)} %all-reduce.11.cloned.1.call-done, pred[128]{0:T(512)(128)(4,1)S(1)} %fusion.49), kind=kOutput, calls=%fused_computation.31 | convolution fusion | flops 3225436160 | bytes 33620096 | tf_op jit(solution)/shard_map/dot_general | solution.py:140
  867.9 3.4 copy-done.1
  (1690 shorter events, 514.1 us)
Async XLA Ops:
  6.5 7.0 copy-start.3
  6.5 206.0 %all-reduce.5.cloned.1.call-start = ((), (), s32[]{:S(2)}) async-start(), calls=%async_computation | async-start | bytes 262144 | tf_op jit(solution)/shard_map/psum | solution.py:91
  168.5 95.4 %all-reduce.7.cloned.1.call-start = ((), (), s32[]{:S(2)}) async-start(), calls=%async_computation.1 | async-start | bytes 131072 | tf_op jit(solution)/shard_map/psum | solution.py:9
  222.2 570.4 %all-reduce.9.cloned.1.call-start = ((), (), s32[]{:S(2)}) async-start(), calls=%async_computation.2 | async-start | bytes 17039360 | tf_op jit(solution)/shard_map/psum | solution.py:9
  671.5 179.1 %all-reduce.11.cloned.1.call-start = ((), (), s32[]{:S(2)}) async-start(), calls=%async_computation.3 | async-start | bytes 131072 | tf_op jit(solution)/shard_map/psum | solution.py:9
  802.5 5.7 copy-start
  850.6 17.3 %copy-start.2 = (f32[128,128]{1,0:T(8,128)S(1)}, f32[128,128]{1,0:T(8,128)}, u32[]{:S(2)}) copy-start(f32[128,128]{1,0:T(8,128)} %all-reduce.11.cloned.1.call-done) | copy-start | bytes 196612
  867.9 3.4 copy-start.1
Sparse Core Ops, SparseCore 0:
  168.6 43.8 all-reduce.4
  222.3 41.5 all-reduce.6
  671.6 120.9 all-reduce.8
  810.0 40.5 all-reduce.10
where the time goes:
time: 881 us; the launch traced here: 878 us
  local copies, waits for them, and re-layouts  272 us (31%)
  waiting for transfers between devices  246 us (28%)
  other arithmetic  184 us (21%)
  matrix products  149 us (17%)
  loops' own time  13.9 us (2%)
  between operations  13.3 us (2%)
    psum x3, waiting for transfers between devices, from_root(): return lax.psum(kept, axis)  202 us
    dot_general x128, matrix products, row_step(): jnp.dot(up_row, upper_inv, precision=lax.Precision.HIGHEST, preferred_ele...  90.9 us
    dynamic_slice x128, local copies, waits for them, and re-layouts, reduce_step(): pivot_value = factors[column_no, column_no]  74.4 us
    dynamic_slice x128, local copies, waits for them, and re-layouts, back_step(): partner = pivots[column_no]  74.2 us
    dynamic_slice x128, local copies, waits for them, and re-layouts, row_step(): lax.dynamic_index_in_dim(diag_values, up_no, 0, keepdims=False)  74.2 us
    broadcast_in_dim x128, other arithmetic, reduce_step(): jnp.where(below[:, None] & (positions[None, :] == column_no), multiplier[...  72.6 us
    select_n x128, other arithmetic, back_step(): jnp.where(sources == column_no, partner, jnp.where(sources == partner, co...  72.6 us
    psum x1, waiting for transfers between devices, swap_rows(): moved_rows = lax.psum(contrib, 'prow')  43.9 us
  transfers between devices with their start and end apart: 4, of which 4 were waited for; matrix products, arithmetic and copies ran while one was open for 0% of the time, Pallas kernels for 0%

commit v1 on v0

--- a/solution.py
+++ b/solution.py
@@ -88,7 +88,11 @@
     source_local = sources // (block_size * prow_count) * block_size + sources % block_size
     fetched = jnp.take(held, jnp.where(source_mine, source_local, 0), axis=0)
     contrib = jnp.where(source_mine[:, None], fetched, 0.0)
-    moved_rows = lax.psum(contrib, "prow")
+    moved_rows = contrib
+    for hop in (1, 2):
+        moved_rows = moved_rows + lax.ppermute(
+            moved_rows, "prow", [(dev, dev ^ hop) for dev in range(4)]
+        )
     target_mine = targets // block_size % prow_count == my_prow
     target_local = targets // (block_size * prow_count) * block_size + targets % block_size
     held = held.at[jnp.where(target_mine, target_local, rows_local)].set(moved_rows, mode="drop")

time: 881 us -> 850 us (0.965)
  waiting for transfers between devices: 246 us -> 211 us
    psum x1 -> x0, waiting for transfers between devices: 43.9 us -> none  [swap_rows(): moved_rows = lax.psum(contrib, 'prow')]
  transfers between devices with their start and end apart: 4 -> 5, of which waited for: 4 -> 5; matrix products, arithmetic and copies ran while one was open for 0% -> 0% of each run, Pallas kernels for 0% -> 0%
where the time goes in v1:
time: 850 us; the launch traced here: 847 us
  local copies, waits for them, and re-layouts  264 us (31%)
  waiting for transfers between devices  211 us (25%)
  other arithmetic  191 us (22%)
  matrix products  149 us (18%)
  loops' own time  13.9 us (2%)
  between operations  13.3 us (2%)
    psum x3, waiting for transfers between devices, from_root(): return lax.psum(kept, axis)  204 us
    dot_general x128, matrix products, row_step(): jnp.dot(up_row, upper_inv, precision=lax.Precision.HIGHEST, preferred_ele...  90.9 us
    dynamic_slice x128, local copies, waits for them, and re-layouts, reduce_step(): pivot_value = factors[column_no, column_no]  74.4 us
    dynamic_slice x128, local copies, waits for them, and re-layouts, back_step(): partner = pivots[column_no]  74.2 us
    dynamic_slice x128, local copies, waits for them, and re-layouts, row_step(): lax.dynamic_index_in_dim(diag_values, up_no, 0, keepdims=False)  74.2 us
    broadcast_in_dim x128, other arithmetic, reduce_step(): jnp.where(below[:, None] & (positions[None, :] == column_no), multiplier[...  72.6 us
    select_n x128, other arithmetic, back_step(): jnp.where(sources == column_no, partner, jnp.where(sources == partner, co...  72.6 us
    dot_general x128, matrix products, row_step(): jnp.dot(low_row, lower_inv, precision=lax.Precision.HIGHEST, preferred_el...  20.1 us
  transfers between devices with their start and end apart: 5, of which 5 were waited for; matrix products, arithmetic and copies ran while one was open for 0% of the time, Pallas kernels for 0%

profile of v1, /device:TPU:0, one launch (start us, length us, event | category | flops | bytes accessed | tf_op | source)
XLA Modules:
  0.0 846.8 jit_solution(16616554307704564258)
XLA Ops:
  6.5 7.0 copy.42
  13.6 150.0 %while.53 = (s32[]{:T(128)}, s32[256]{0:T(256)S(1)}, s32[128]{0:T(128)S(1)}, s32[]{:T(128)}, s32[]{:T(128)}, /*index=5*/s32[]{:T(128)}, s32[]{:T(128)}) while((s32[]{:T(128)}, s32[256]{0:T(256)S(1)}, s32[128]{0:T(128)S(1)}, s32[]{:T(128)}, s32[]{:T(128)}, /*index=5*/s32[]{:T(128)}, s32[]{:T(128)}) %tuple.140), condition=%wide.region_1.2_spmd, body=%wide.region_0.1_spmd.sunk | while | flops 1030 | bytes 2191 | solution.py:80
  163.6 4.1 gather_fusion
  167.8 1.7 collective-permute-start
  169.5 3.5 collective-permute-done
  173.1 3.4 collective-permute-start.1
  176.5 3.2 collective-permute-done.1
  179.7 7.9 scatter_custom_fusion
  187.6 1.5 slice_select_fusion.3
  189.2 43.8 %all-reduce.4.cloned.1.call-done = f32[128,128]{1,0:T(8,128)} async-done(((f32[128,128]{1,0:T(8,128)}), f32[128,128]{1,0:T(8,128)}) %all-reduce.4.cloned.1.call-update) | async-done | bytes 65552 | tf_op jit(solution)/shard_map/psum | solution.py:9
  232.9 0.9 copy.4
  233.9 180.8 %while.54 = (s32[]{:T(128)}, f32[128,128]{0,1:T(8,128)S(1)}, s32[]{:T(128)}) while((s32[]{:T(128)}, f32[128,128]{0,1:T(8,128)S(1)}, s32[]{:T(128)}) %tuple.128), condition=%wide.region_5.6_spmd.clone.clone, body=%wide.region_4.5_spmd.clone.clone.sunk | while | flops 66434 | bytes 268349 | solution.py:27
  414.9 197.9 %while.55 = (s32[]{:T(128)}, f32[128,128]{1,0:T(8,128)S(1)}, f32[128,128]{1,0:T(8,128)S(1)}, f32[128,128]{1,0:T(8,128)S(1)}, f32[128]{0:T(128)S(1)}, /*index=5*/...) while((s32[]{:T(128)}, f32[128,128]{1,0:T(8,128)S(1)}, ...), condition=%wide.region_8.9_spmd.clone.clone, body=%wide.region_7.8_spmd.clone.clone.sunk | while | flops 394118 | bytes 136371 | solution.py:63
  612.8 18.9 %convolution_select_fusion = f32[16384,128]{1,0:T(8,128)S(1)} fusion(f32[16384,128]{1,0:T(8,128)} %scatter_custom_fusion, f32[128,128]{1,0:T(8,128)S(1)} %get-tuple-element.386, pred[16384]{0:T(1024)(128)(4,1)S(1)} %fusion.31), kind=kOutput, calls=%fused_computation.32 | convolution fusion | flops 3223322624 | bytes 16859136 | tf_op jit(solution)/shard_map/dot_general | solution.py:130
  631.8 8.8 %maximum_select_fusion = f32[16640,128]{1,0:T(8,128)} fusion(f32[128,128]{1,0:T(8,128)S(1)} %get-tuple-element.387, f32[128,128]{1,0:T(8,128)S(1)} %copy.5, f32[16384,128]{1,0:T(8,128)S(1)} %convolution_select_fusion, pred[]{:T(512)S(6)} %eq.133), kind=kLoop, calls=%fused_computation.33 | loop fusion | flops 6389760 | bytes 17039360 | tf_op jit(solution)/shard_map/jit(_where)/select_n | solution.py:8
  640.8 120.8 %all-reduce.6.cloned.1.call-done = f32[16640,128]{1,0:T(8,128)} async-done(((f32[16640,128]{1,0:T(8,128)}), f32[16640,128]{1,0:T(8,128)}) %all-reduce.6.cloned.1.call-update) | async-done | bytes 8519696 | tf_op jit(solution)/shard_map/psum | solution.py:9
  761.6 9.8 %slice_select_fusion = f32[16384,128]{1,0:T(8,128)S(1)} fusion(f32[16384,128]{1,0:T(8,128)} %scatter_custom_fusion, f32[16640,128]{1,0:T(8,128)} %all-reduce.6.cloned.1.call-done, pred[16384]{0:T(1024)(128)(4,1)S(1)} %fusion.31), kind=kLoop, calls=%fused_computation.35 | loop fusion | flops 2097152 | bytes 25182208 | tf_op jit(solution)/shard_map/jit(_where)/select_n | solution.py:147
  771.5 3.3 copy.38
  774.8 2.4 copy-done
  777.2 1.7 convolution_select_fusion.1
  778.9 1.5 fusion.36
  780.4 39.2 %all-reduce.8.cloned.1.call-done = f32[128,128]{1,0:T(8,128)} async-done(((f32[128,128]{1,0:T(8,128)}), f32[128,128]{1,0:T(8,128)}) %all-reduce.8.cloned.1.call-update) | async-done | bytes 65552 | tf_op jit(solution)/shard_map/psum | solution.py:9
  819.6 17.2 %fusion.17 = f32[16384,128]{1,0:T(8,128)S(1)} fusion(f32[16384,128]{1,0:T(8,128)} %bitcast.90, f32[16384,128]{1,0:T(8,128)} %scatter_custom_fusion, f32[16640,128]{1,0:T(8,128)} %all-reduce.6.cloned.1.call-done, pred[]{:T(512)S(6)} %eq.133, f32[128,128]{1,0:T(8,128)} %all-reduce.8.cloned.1.call-done, pred[128]{0:T(512)(128)(4,1)S(1)} %fusion.51), kind=kOutput, calls=%fused_computation.31 | convolution fusion | flops 3225436160 | bytes 33620096 | tf_op jit(solution)/shard_map/dot_general | solution.py:144
  836.9 3.4 copy-done.1
  (1692 shorter events, 515.7 us)
Async XLA Ops:
  6.5 7.0 copy-start.3
  6.5 226.4 %all-reduce.4.cloned.1.call-start = ((), (), s32[]{:S(2)}) async-start(), calls=%async_computation | async-start | bytes 131072 | tf_op jit(solution)/shard_map/psum | solution.py:9
  167.8 5.2 collective-permute-start
  173.1 6.6 collective-permute-start.1
  189.1 572.5 %all-reduce.6.cloned.1.call-start = ((), (), s32[]{:S(2)}) async-start(), calls=%async_computation.1 | async-start | bytes 17039360 | tf_op jit(solution)/shard_map/psum | solution.py:9
  640.5 179.1 %all-reduce.8.cloned.1.call-start = ((), (), s32[]{:S(2)}) async-start(), calls=%async_computation.2 | async-start | bytes 131072 | tf_op jit(solution)/shard_map/psum | solution.py:9
  771.5 5.7 copy-start
  819.6 17.3 %copy-start.2 = (f32[128,128]{1,0:T(8,128)S(1)}, f32[128,128]{1,0:T(8,128)}, u32[]{:S(2)}) copy-start(f32[128,128]{1,0:T(8,128)} %all-reduce.8.cloned.1.call-done) | copy-start | bytes 196612
  836.9 3.4 copy-start.1
Sparse Core Ops, SparseCore 0:
  189.2 43.7 all-reduce.3
  640.7 120.9 all-reduce.5
  779.0 40.5 all-reduce.7
